TPU v7x, 256 devices: a whole 4x4x8 slice. The times are simulated.
256 devices in a mesh: row: 16 (over z, core), col: 4 (over x), seed: 4 (over y).
Axes of the slice: x: 4, y: 4, z: 8, core: 2. Of those that a mesh axis runs over, the one named last changes fastest.
Arguments:
- tiles: bfloat16 [16, 4, 384, 128, 128], P('row', 'col'), may hold values from -0.0390625 to 0.0390625
- tile_out: int32 [16, 4, 384], P('row', 'col'), may hold values from 0 to 15, as said below
- tile_in: int32 [16, 4, 384], P('row', 'col'), may hold values from 0 to 3
- tile_count: int32 [16, 4], P('row', 'col'), may hold values from 1 to 384, as said below
- out_degree: int32 [8192], P(('row', 'col')), may hold values from 1 to 8
- seed_ids: int32 [512, 16], P('seed'), may hold values from 0 to 8191
- prior: float32 [512, 8192], P('seed', ('row', 'col')), may hold values from -6 to 6
Outputs:
- risk: float32 [512, 8192], P('seed', ('row', 'col'))
Inputs may be any that keep to these rules, and one draw needn't show every extreme that they name: `tile_count`: occupied slots of a device come first; some device has all 384 occupied in every draw. `tile_out`: on every device the output blocks named by the occupied slots never fall from one slot to the next; several occupied slots of one device may name the same output block, and the same pair of blocks.
All inputs are finite; a program needn't handle non-finite values.
Results may differ from a plain program's by a relative error of at most 0.0041.
Values may be sent and summed in bfloat16 or wider, within the bound.
A program may use at most 64 MiB of HBM per device.

v0:
```python
import math

import jax
import jax.numpy as jnp
from jax import lax
from jax.sharding import PartitionSpec as P

ITERATIONS = 2


damping = 0.85


def products(blocks, tiles_here, out_ids, in_ids, first_slot, end_slot, base_block, block_total):
    slot_total = tiles_here.shape[0]
    group_size = math.gcd(slot_total, 32)
    sets_here = blocks.shape[1]
    block_edge = tiles_here.shape[2]
    offsets = jnp.arange(group_size, dtype=jnp.int32)
    first_group = first_slot // group_size
    end_group = (end_slot + group_size - 1) // group_size

    def advance(group_index, panel_sum):
        slot_start = group_index * group_size
        tile_block = lax.dynamic_slice_in_dim(tiles_here, slot_start, group_size, 0)
        targets = lax.dynamic_slice_in_dim(out_ids, slot_start, group_size, 0) - base_block
        sources = lax.dynamic_slice_in_dim(in_ids, slot_start, group_size, 0)
        gathered = jnp.take(blocks, sources, axis=0)
        product = jnp.einsum(
            "gsk,gkj->gsj", gathered, tile_block, preferred_element_type=jnp.float32
        )
        slot_here = slot_start + offsets
        valid_mask = ((slot_here >= first_slot) & (slot_here < end_slot)).astype(jnp.float32)
        targets = jnp.clip(targets, 0, block_total - 1)
        return panel_sum.at[targets].add(product * valid_mask[:, None, None])

    zero_panel = jnp.zeros((block_total, sets_here, block_edge), jnp.float32)
    return lax.fori_loop(first_group, end_group, advance, zero_panel)


def local(tiles, tile_out, tile_in, tile_count, out_degree, seed_ids, prior):
    tiles_here = tiles[0, 0]
    out_ids = tile_out[0, 0]
    in_ids = tile_in[0, 0]
    occupied = tile_count[0, 0]
    row_devices = lax.axis_size("row")
    col_devices = lax.axis_size("col")
    sets_here, owned_count = prior.shape
    block_edge = tiles_here.shape[1]
    owned_blocks = owned_count // block_edge
    out_blocks = row_devices * owned_blocks
    own_start = (lax.axis_index("row") * col_devices + lax.axis_index("col")) * owned_count
    local_ids = seed_ids - own_start
    positions = jnp.arange(owned_count, dtype=jnp.int32)
    restart_rows = jnp.sum(
        (local_ids[:, :, None] == positions[None, None, :]).astype(jnp.float32), axis=1
    )
    restart = restart_rows.reshape(sets_here, owned_blocks, block_edge).transpose(1, 0, 2)
    degree = out_degree.astype(jnp.float32).reshape(owned_blocks, 1, block_edge)
    risk_now = prior.reshape(sets_here, owned_blocks, block_edge).transpose(1, 0, 2)
    for round_index in range(ITERATIONS):
        scaled = (risk_now / degree).astype(jnp.bfloat16)
        blocks = lax.all_gather(scaled, "col", axis=0, tiled=True)
        partial_value = products(blocks, tiles_here, out_ids, in_ids, 0, occupied, 0, out_blocks)
        incoming = lax.psum_scatter(partial_value, "row", scatter_dimension=0, tiled=True)
        risk_now = (1.0 - damping) * restart + damping * incoming
    return risk_now.transpose(1, 0, 2).reshape(sets_here, owned_count)


def solution(mesh):
    placed = (
        P("row", "col", None, None, None),
        P("row", "col", None),
        P("row", "col", None),
        P("row", "col"),
        P(("row", "col")),
        P("seed", None),
        P("seed", ("row", "col")),
    )
    return jax.shard_map(
        local, mesh=mesh, in_specs=placed, out_specs=P("seed", ("row", "col")), check_vma=False
    )
```

profile of v0, /device:TPU:1, one launch (start us, length us, event | category | flops | bytes accessed | tf_op | source)
XLA Modules:
  0.0 331.9 jit_solution(5670135569856032543)
XLA Ops:
  8.7 10.3 %all-gather = bf16[512,128]{1,0:T(8,128)(2,1)S(1)} all-gather(bf16[128,128]{1,0:T(8,128)(2,1)S(1)} %divide_convert_fusion), channel_id=2, replica_groups=mesh['row'=16,'col'=4,'seed'=4] {'col'}, dimensions={0}, use_global_device_ids=true | all-gather | bytes 163840 | tf_op jit(solution)/shard_map/all_gather | solution.py:63
  20.5 86.5 %while.22 = (s32[]{:T(128)}, f32[16,128,128]{2,1,0:T(8,128)S(1)}, s32[]{:T(128)}, s32[384]{0:T(512)S(1)}, s32[384]{0:T(512)S(1)}, /*index=5*/bf16[4,128,128]{2,1...) while((s32[]{:T(128)}, f32[16,128,128]{2,1,0:T(8,128)S(1)}, ...), condition=%wide.region_3.5_spmd.clone, body=%wide.region_1.4_spmd.clone.sunk | while | flops 135792096 | bytes 12588407 | solution.py:38
  23.0 2.0 convolution_multiply_fusion.4
  25.1 2.7 scatter_fusion
  32.3 2.7 scatter_fusion
  37.4 2.0 convolution_multiply_fusion.4
  39.5 2.7 scatter_fusion
  44.6 2.0 convolution_multiply_fusion.4
  46.7 2.7 scatter_fusion
  51.8 2.0 convolution_multiply_fusion.4
  53.9 2.7 scatter_fusion
  59.0 2.0 convolution_multiply_fusion.4
  61.1 2.7 scatter_fusion
  68.4 2.7 scatter_fusion
  75.6 2.7 scatter_fusion
  80.7 2.0 convolution_multiply_fusion.4
  82.8 2.7 scatter_fusion
  87.9 2.0 convolution_multiply_fusion.4
  90.0 2.7 scatter_fusion
  97.2 2.7 scatter_fusion
  102.3 2.0 convolution_multiply_fusion.4
  104.4 2.7 scatter_fusion
  108.7 58.9 %reduce-scatter.3.cloned.1.call-done = f32[1,128,128]{2,1,0:T(8,128)} async-done(((f32[16,128,128]{2,1,0:T(8,128)}), f32[1,128,128]{2,1,0:T(8,128)}) %reduce-scatter.3.cloned.1.call-update) | async-done | bytes 65552 | tf_op jit(solution)/shard_map/reduce_scatter | solution.py:65
  168.5 9.3 %all_gather.7 = bf16[4,128,128]{2,1,0:T(8,128)(2,1)S(1)} all-gather(bf16[1,128,128]{2,1,0:T(8,128)(2,1)S(1)} %fusion.17), channel_id=1, replica_groups=mesh['row'=16,'col'=4,'seed'=4] {'col'}, dimensions={0}, use_global_device_ids=true | all-gather | bytes 163840 | tf_op jit(solution)/shard_map/all_gather | solution.py:63
  177.8 86.6 %while.23 = (s32[]{:T(128)}, f32[16,128,128]{2,1,0:T(8,128)S(1)}, s32[]{:T(128)}, s32[384]{0:T(512)S(1)}, s32[384]{0:T(512)S(1)}, /*index=5*/bf16[4,128,128]{2,1...) while((s32[]{:T(128)}, f32[16,128,128]{2,1,0:T(8,128)S(1)}, ...), condition=%wide.region_7.9_spmd.clone, body=%wide.region_5.8_spmd.clone.sunk | while | flops 135792096 | bytes 12588407 | solution.py:38
  182.4 2.7 scatter_fusion.1
  187.5 2.0 convolution_multiply_fusion.5
  189.6 2.7 scatter_fusion.1
  194.7 2.0 convolution_multiply_fusion.5
  196.8 2.7 scatter_fusion.1
  201.9 2.0 convolution_multiply_fusion.5
  204.0 2.7 scatter_fusion.1
  209.1 2.0 convolution_multiply_fusion.5
  211.2 2.7 scatter_fusion.1
  216.3 2.0 convolution_multiply_fusion.5
  218.5 2.7 scatter_fusion.1
  223.5 2.0 convolution_multiply_fusion.5
  225.7 2.7 scatter_fusion.1
  230.8 2.0 convolution_multiply_fusion.5
  232.9 2.7 scatter_fusion.1
  238.0 2.0 convolution_multiply_fusion.5
  240.1 2.7 scatter_fusion.1
  247.3 2.7 scatter_fusion.1
  252.4 2.0 convolution_multiply_fusion.5
  254.5 2.7 scatter_fusion.1
  259.6 2.0 convolution_multiply_fusion.5
  261.7 2.7 scatter_fusion.1
  265.4 58.1 %reduce-scatter.5.cloned.1.call-done = f32[1,128,128]{2,1,0:T(8,128)} async-done(((f32[16,128,128]{2,1,0:T(8,128)}), f32[1,128,128]{2,1,0:T(8,128)}) %reduce-scatter.5.cloned.1.call-update) | async-done | bytes 65552 | tf_op jit(solution)/shard_map/reduce_scatter | solution.py:65
  (123 shorter events, 79.8 us)
Async XLA Ops:
  6.5 161.1 %reduce-scatter.3.cloned.1.call-start = ((), (), s32[]{:S(2)}) async-start(), calls=%async_computation.2 | async-start | bytes 1114112 | tf_op jit(solution)/shard_map/reduce_scatter | solution.py:65
  20.5 87.6 %copy-start.2 = (s32[128,16]{0,1:T(8,128)S(1)}, s32[128,16]{0,1:T(8,128)}, u32[]{:S(2)}) copy-start(s32[128,16]{0,1:T(8,128)} %param.18) | copy-start | bytes 24580
  107.1 1.0 copy-start.1
  108.1 215.4 %reduce-scatter.5.cloned.1.call-start = ((), (), s32[]{:S(2)}) async-start(), calls=%async_computation.3 | async-start | bytes 1114112 | tf_op jit(solution)/shard_map/reduce_scatter | solution.py:65
  264.4 1.0 copy-start
Sparse Core Ops, SparseCore 0:
  108.2 59.3 reduce-scatter.2
  265.5 57.9 reduce-scatter.4
where the time goes:
time: 335 us; the launch traced here: 332 us
  waiting for transfers between devices  117 us (35%)
  other arithmetic  88.9 us (27%)
  matrix products  48.7 us (15%)
  local copies, waits for them, and re-layouts  42.4 us (13%)
  blocking collectives  19.6 us (6%)
  between operations  14.2 us (4%)
    reduce_scatter x2, waiting for transfers between devices, local(): lax.psum_scatter(partial_value, 'row', scatter_dimension=0, tiled=True)  117 us
    scatter-add x24, other arithmetic, advance(): return panel_sum.at[targets].add(product * valid_mask[:, None, None])  63.7 us
    dot_general x24, matrix products, advance(): jnp.einsum('gsk,gkj->gsj', gathered, tile_block, preferred_element_type=j...  48.7 us
    gather x24, local copies, waits for them, and re-layouts, advance(): gathered = jnp.take(blocks, sources, axis=0)  40.1 us
    all_gather x2, blocking collectives, local(): blocks = lax.all_gather(scaled, 'col', axis=0, tiled=True)  19.6 us
    and x24, other arithmetic, advance(): gathered = jnp.take(blocks, sources, axis=0)  17.5 us
  transfers between devices with their start and end apart: 2, of which 2 were waited for; matrix products, arithmetic and copies ran while one was open for 0% of the time, Pallas kernels for 0%

commit v1 on v0

v1 whole, which is shorter than its diff:
```python
import functools
import math

import jax
import jax.numpy as jnp
from jax import lax
from jax.experimental import pallas as pl
from jax.experimental.pallas import tpu as pltpu
from jax.sharding import PartitionSpec as P

ITERATIONS = 2
PARTS = 4
damping = 0.85
MESH = pl.DeviceIdType.MESH


def ring_order(ring):
    return sorted(range(ring), key=lambda d: -min(d, ring - d))


def kernel(
    rows, cols, chunks,
    count, outs, ins, tiles, degree, seeds, prior, risk_out,
    buf, sum0, sum1, sum2, sum3, heads, w, xs, own, psend, precv, zsend, zrecv,
    tsem, xs_send, xs_recv, ps_send, ps_recv, zs_send, zs_recv,
):
    sums = (sum0, sum1, sum2, sum3)
    slots, edge, _ = buf.shape
    group = slots // chunks
    part = edge // PARTS
    ring = rows // 2
    row = lax.axis_index("row")
    col = lax.axis_index("col")
    core = lax.rem(row, 2)
    chip = row // 2
    partner = row + 1 - 2 * core
    depth = cols * edge
    order = ring_order(ring)
    none = slots

    def tile_copy(g):
        at = pl.ds(g * group, group)
        return pltpu.make_async_copy(tiles.at[at], buf.at[at], tsem.at[g])

    barrier = pltpu.get_barrier_semaphore()
    for d in range(1, cols):
        pl.semaphore_signal(barrier, inc=1, device_id={"col": lax.rem(col + d, cols)}, device_id_type=MESH)
    pl.semaphore_signal(barrier, inc=1, device_id={"row": partner}, device_id_type=MESH)
    for d in range(1, ring):
        peer = lax.rem(chip + d, ring) * 2 + core
        pl.semaphore_signal(barrier, inc=1, device_id={"row": peer}, device_id_type=MESH)
    for g in range(chunks):
        tile_copy(g).start()

    degrees = degree[...].astype(jnp.float32)

    def gather(step, risk):
        xs[step, col] = (risk / degrees).astype(jnp.bfloat16)
        copies = []
        for d in range(1, cols):
            copy = pltpu.make_async_remote_copy(
                src_ref=xs.at[step, col],
                dst_ref=xs.at[step, col],
                send_sem=xs_send.at[step, d - 1],
                recv_sem=xs_recv.at[step, d - 1],
                device_id={"col": lax.rem(col + d, cols)},
                device_id_type=MESH,
            )
            copies.append(copy)
        return copies

    first_copies = gather(0, prior[...])
    pl.semaphore_wait(barrier, cols - 1 + 1 + ring - 1)
    for copy in first_copies:
        copy.start()

    for q in range(PARTS):
        sums[q][none] = jnp.zeros((part, edge), jnp.float32)

    def add_tile(s, carry):
        last_out, last_in = carry[0], carry[1:]
        o = outs[s]
        i = ins[s]
        same = o == last_out
        last_in = [jnp.where(same, h, none) for h in last_in]
        prev = last_in[0]
        for k in range(1, cols):
            prev = jnp.where(i == k, last_in[k], prev)
        for q in range(PARTS):
            tile = buf[s, q * part:(q + 1) * part, :].astype(jnp.float32)
            sums[q][s] = sums[q][prev] + tile
        last_in = [jnp.where(i == k, s, last_in[k]) for k in range(cols)]
        for k in range(0, cols, 2):
            heads[k // 2, s] = last_in[k] + last_in[k + 1] * 65536
        return (o, *last_in)

    carry = (jnp.int32(-1),) + (jnp.int32(none),) * cols
    for g in range(chunks):
        tile_copy(g).wait()
        carry = lax.fori_loop(g * group, (g + 1) * group, add_tile, carry, unroll=4)

    used = count[0]
    steps = [1 << b for b in reversed(range(slots.bit_length()))]

    def last_slots(o):
        end = jnp.int32(0)
        for step in steps:
            mid = end + step
            inside = mid <= used
            fits = outs[jnp.minimum(mid, slots) - 1] <= o
            end = jnp.where(inside & fits, mid, end)
        at = jnp.maximum(end - 1, 0)
        hit = (end > 0) & (outs[at] == o)
        found = []
        for k in range(0, cols, 2):
            pair = heads[k // 2, at]
            found.append(jnp.where(hit, pair % 65536, none))
            found.append(jnp.where(hit, pair // 65536, none))
        return found

    def build(n, target):
        for half in range(2):
            places = last_slots(target * 2 + half)
            for k in range(cols):
                for q in range(PARTS):
                    value = sums[q][places[k]]
                    high = value.astype(jnp.bfloat16)
                    low = (value - high.astype(jnp.float32)).astype(jnp.bfloat16)
                    at = k * edge + q * part
                    w[n, at:at + part, half * edge:(half + 1) * edge] = high
                    w[n, depth + at:depth + at + part, half * edge:(half + 1) * edge] = low

    start = (row * cols + col) * edge
    restart = None
    incoming = None
    for step in range(ITERATIONS):
        copies = first_copies if step == 0 else gather(step, risk)
        if step > 0:
            for copy in copies:
                copy.start()
        for copy in copies:
            copy.wait()
        parts = [xs[step, k] for k in range(cols)]
        x = jnp.concatenate(parts + parts, axis=1)
        partner_copies = []
        for n, d in enumerate(order):
            target = lax.rem(chip + d, ring)
            if step == 0:
                build(n, target)
            both = jnp.dot(x, w[n], preferred_element_type=jnp.float32)
            left, right = both[:, :edge], both[:, edge:]
            psend[step, n] = jnp.where(core == 0, right, left).astype(jnp.bfloat16)
            copy = pltpu.make_async_remote_copy(
                src_ref=psend.at[step, n],
                dst_ref=precv.at[step, n],
                send_sem=ps_send.at[step, n],
                recv_sem=ps_recv.at[step, n],
                device_id={"row": partner},
                device_id_type=MESH,
            )
            copy.start()
            partner_copies.append(copy)
            own[n] = jnp.where(core == 0, left, right)
        chip_copies = []
        for n, d in enumerate(order):
            partner_copies[n].wait()
            total = own[n] + precv[step, n].astype(jnp.float32)
            if d == 0:
                incoming = total
            else:
                zsend[step, n] = total.astype(jnp.bfloat16)
                copy = pltpu.make_async_remote_copy(
                    src_ref=zsend.at[step, n],
                    dst_ref=zrecv.at[step, n],
                    send_sem=zs_send.at[step, n],
                    recv_sem=zs_recv.at[step, n],
                    device_id={"row": lax.rem(chip + d, ring) * 2 + core},
                    device_id_type=MESH,
                )
                copy.start()
                chip_copies.append((n, copy))
        if step == 0:
            local_ids = seeds[...] - start
            places = lax.broadcasted_iota(jnp.int32, (local_ids.shape[0], edge), 1)
            restart = jnp.zeros(places.shape, jnp.float32)
            for j in range(local_ids.shape[1]):
                restart += (local_ids[:, j:j + 1] == places).astype(jnp.float32)
        for n, copy in reversed(chip_copies):
            copy.wait()
            incoming += zrecv[step, n].astype(jnp.float32)
        risk = (1.0 - damping) * restart + damping * incoming
    risk_out[...] = risk


def local(tiles, tile_out, tile_in, tile_count, out_degree, seed_ids, prior):
    rows, cols = lax.axis_size("row"), lax.axis_size("col")
    slots, edge = tiles.shape[2], tiles.shape[4]
    sets = prior.shape[0]
    ring = rows // 2
    chunks = math.gcd(slots, 8)
    vmem = pl.BlockSpec(memory_space=pltpu.VMEM)
    smem = pl.BlockSpec(memory_space=pltpu.SMEM)
    hbm = pl.BlockSpec(memory_space=pl.ANY)
    block = (sets, edge)
    dma = pltpu.SemaphoreType.DMA
    return pl.pallas_call(
        functools.partial(kernel, rows, cols, chunks),
        out_shape=jax.ShapeDtypeStruct(block, jnp.float32),
        in_specs=[smem, smem, smem, hbm, vmem, vmem, vmem],
        out_specs=vmem,
        scratch_shapes=[
            pltpu.VMEM((slots, edge, edge), jnp.bfloat16),
            *[pltpu.VMEM((slots + 1, edge // PARTS, edge), jnp.float32) for _ in range(PARTS)],
            pltpu.SMEM((cols // 2, slots), jnp.int32),
            pltpu.VMEM((ring, 2 * cols * edge, 2 * edge), jnp.bfloat16),
            pltpu.VMEM((ITERATIONS, cols, *block), jnp.bfloat16),
            pltpu.VMEM((ring, *block), jnp.float32),
            pltpu.VMEM((ITERATIONS, ring, *block), jnp.bfloat16),
            pltpu.VMEM((ITERATIONS, ring, *block), jnp.bfloat16),
            pltpu.VMEM((ITERATIONS, ring, *block), jnp.bfloat16),
            pltpu.VMEM((ITERATIONS, ring, *block), jnp.bfloat16),
            dma((chunks,)),
            dma((ITERATIONS, cols)),
            dma((ITERATIONS, cols)),
            dma((ITERATIONS, ring)),
            dma((ITERATIONS, ring)),
            dma((ITERATIONS, ring)),
            dma((ITERATIONS, ring)),
        ],
        compiler_params=pltpu.CompilerParams(
            collective_id=0, has_side_effects=True, vmem_limit_bytes=60 * 1024 * 1024
        ),
    )(
        tile_count.reshape(1),
        tile_out.reshape(slots),
        tile_in.reshape(slots),
        tiles.reshape(slots, edge, edge),
        out_degree.reshape(1, edge),
        seed_ids,
        prior,
    )


def solution(mesh):
    placed = (
        P("row", "col", None, None, None),
        P("row", "col", None),
        P("row", "col", None),
        P("row", "col"),
        P(("row", "col")),
        P("seed", None),
        P("seed", ("row", "col")),
    )
    return jax.shard_map(
        local, mesh=mesh, in_specs=placed, out_specs=P("seed", ("row", "col")), check_vma=False
    )
```

time: 335 us -> 48.4 us (0.14)
  waiting for transfers between devices: 117 us -> 0 us
  other arithmetic: 88.9 us -> 2.53 us
  matrix products: 48.7 us -> 0 us
  Pallas kernels: 0 us -> 42 us
  local copies, waits for them, and re-layouts: 42.4 us -> 2.9 us
  blocking collectives: 19.6 us -> 0 us
  between operations: 14.2 us -> 0.66 us
    reduce_scatter x2 -> x0, waiting for transfers between devices: 117 us -> none  [local(): lax.psum_scatter(partial_value, 'row', scatter_dimension=0, tiled=True)]
    scatter-add x24 -> x0, other arithmetic: 63.7 us -> none  [advance(): return panel_sum.at[targets].add(product * valid_mask[:, None, None])]
    dot_general x24 -> x0, matrix products: 48.7 us -> none  [advance(): jnp.einsum('gsk,gkj->gsj', gathered, tile_block, preferred_element_type=j...]
    pallas_call x0 -> x1, Pallas kernels: none -> 42 us  [local(): pl.pallas_call(functools.partial(kernel, rows, cols, chunks), out_shape=j...]
    gather x24 -> x0, local copies, waits for them, and re-layouts: 40.1 us -> none  [advance(): gathered = jnp.take(blocks, sources, axis=0)]
    all_gather x2 -> x0, blocking collectives: 19.6 us -> none  [local(): blocks = lax.all_gather(scaled, 'col', axis=0, tiled=True)]
    and x24 -> x0, other arithmetic: 17.5 us -> none  [advance(): gathered = jnp.take(blocks, sources, axis=0)]
  transfers between devices with their start and end apart: 2 -> 0, of which waited for: 2 -> 0; matrix products, arithmetic and copies ran while one was open for 0% -> 0% of each run, Pallas kernels for 0% -> 0%
where the time goes in v1:
time: 48.4 us; the launch traced here: 48.1 us
  Pallas kernels  42 us (87%)
  local copies, waits for them, and re-layouts  2.9 us (6%)
  other arithmetic  2.53 us (5%)
  between operations  0.66 us (1%)
    pallas_call x1, Pallas kernels, local(): pl.pallas_call(functools.partial(kernel, rows, cols, chunks), out_shape=j...  42 us
    unnamed x2, local copies, waits for them, and re-layouts  2.9 us
    unnamed x2, other arithmetic  2.53 us

profile of v1, /device:TPU:1, one launch (start us, length us, event | category | flops | bytes accessed | tf_op | source)
XLA Modules:
  0.0 48.1 jit_solution(8924752351388854964)
XLA Ops:
  0.7 1.3 %reduce.outs = s32[384]{0:T(512)} reduce(s32[1,1,384]{2,1,0:T(1,128)} %param.8, s32[]{:T(128)} %constant.4), dimensions={0,1}, to_apply=%param.8.reduce_sub_computation | reduce | bytes 3076 | tf_op args[1]
  1.9 1.3 %reduce.1.ins = s32[384]{0:T(512)} reduce(s32[1,1,384]{2,1,0:T(1,128)} %param.9, s32[]{:T(128)} %constant.4), dimensions={0,1}, to_apply=%param.9.reduce_sub_computation | reduce | bytes 3076 | tf_op args[2]
  3.2 1.4 %copy.8.seeds = s32[128,16]{1,0:T(8,128)} copy(s32[128,16]{0,1:T(8,128)} %param.12) | data formatting | bytes 16384 | tf_op args[5]
  4.6 42.0 %shard_map.73 = f32[128,128]{1,0:T(8,128)} custom-call(s32[1]{0:T(128)} %bitcast.3.count, s32[384]{0:T(512)} %reduce.outs, s32[384]{0:T(512)} %reduce.1.ins, bf16[384,128,128]{2,1,0:T(8,128)(2,1)} %bitcast.4, s32[1,128]{1,0:T(1,128)} %bitcast.5, s32[128,16]{1,0:T(8,128)} %copy.8.seeds, f32[128,128]{1,0:T(8,128)} %prior.1), custom_call_target="tpu_custom_call" | custom-call | tf_op jit(solution)/shard_map/pallas_call | solution.py:206
  46.6 1.5 %copy.11 = f32[128,128]{1,0:T(8,128)} copy(f32[128,128]{1,0:T(8,128)} %shard_map.73) | data formatting | bytes 131072

commit v2 on v1

v2 whole, which is shorter than its diff:
```python
import functools
import math

import jax
import jax.numpy as jnp
from jax import lax
from jax.experimental import pallas as pl
from jax.experimental.pallas import tpu as pltpu
from jax.sharding import PartitionSpec as P

ITERATIONS = 2
PARTS = 4
CHUNKS = 16
FLIGHT = 4
HALVES = 2
X_CHUNK = 2
Z_CHUNK = 12
LAG_FIRST = 3
LAG_LAST = 5
damping = 0.85
MESH = pl.DeviceIdType.MESH


def ring_order(ring):
    return sorted(range(ring), key=lambda d: -min(d, ring - d))


def kernel(
    rows, cols, chunks,
    count, outs_in, ins_in, tiles, degree_in, seeds_in, prior_in, risk_out,
    outs, ins, degree, seeds, prior, buf, sum0, sum1, sum2, sum3, heads,
    w, xs, own, psend, precv, zsend, zrecv,
    isem, tsem, xs_send, xs_recv, ps_send, ps_recv, zs_send, zs_recv, x_ready, z_ready,
):
    sums = (sum0, sum1, sum2, sum3)
    slots, edge, _ = buf.shape
    sets = prior.shape[0]
    size = sets // HALVES
    group = slots // chunks
    part = edge // PARTS
    ring = rows // 2
    row = lax.axis_index("row")
    col = lax.axis_index("col")
    core = lax.rem(row, 2)
    chip = row // 2
    partner = row + 1 - 2 * core
    depth = cols * edge
    order = ring_order(ring)
    none = slots
    sent = []

    def tile_copy(g):
        at = pl.ds(g * group, group)
        return pltpu.make_async_copy(tiles.at[at], buf.at[at], tsem.at[g])

    def send(source, target, send_sem, recv_sem, device):
        copy = pltpu.make_async_remote_copy(
            src_ref=source, dst_ref=target, send_sem=send_sem, recv_sem=recv_sem,
            device_id=device, device_id_type=MESH,
        )
        copy.start()
        sent.append(copy)
        return copy

    small = [
        pltpu.make_async_copy(source, place, isem.at[n])
        for n, (source, place) in enumerate((
            (degree_in, degree), (prior_in, prior), (outs_in, outs), (ins_in, ins), (seeds_in, seeds),
        ))
    ]
    for copy in small:
        copy.start()
    for g in range(FLIGHT):
        tile_copy(g).start()

    barrier = pltpu.get_barrier_semaphore()
    for d in range(1, cols):
        pl.semaphore_signal(
            barrier, inc=1, device_id={"row": chip * 2, "col": lax.rem(col + d, cols)}, device_id_type=MESH
        )
    pl.semaphore_signal(barrier, inc=1, device_id={"row": partner}, device_id_type=MESH)
    for d in range(1, ring):
        peer = lax.rem(chip + d, ring) * 2 + 1
        pl.semaphore_signal(barrier, inc=1, device_id={"row": peer}, device_id_type=MESH)

    small[0].wait()
    small[1].wait()
    degrees = degree[...].astype(jnp.float32)

    def gather(step, half, at, length):
        rows_at = pl.ds(at, length)
        return [
            send(
                xs.at[step, col, rows_at], xs.at[step, col, rows_at],
                xs_send.at[step, half, d - 1], xs_recv.at[step, half, d - 1],
                {"col": lax.rem(col + d, cols)},
            )
            for d in range(1, cols)
        ]

    xs[0, col] = (prior[...] / degrees).astype(jnp.bfloat16)
    for copy in small[2:]:
        copy.wait()
    for q in range(PARTS):
        sums[q][none] = jnp.zeros((part, edge), jnp.float32)

    def add_tile(s, carry):
        last_out, last_in = carry[0], carry[1:]
        o = outs[0, 0, s]
        i = ins[0, 0, s]
        same = o == last_out
        last_in = [jnp.where(same, h, none) for h in last_in]
        prev = last_in[0]
        for k in range(1, cols):
            prev = jnp.where(i == k, last_in[k], prev)
        for q in range(PARTS):
            tile = buf[s, q * part:(q + 1) * part, :].astype(jnp.float32)
            sums[q][s] = sums[q][prev] + tile
        last_in = [jnp.where(i == k, s, last_in[k]) for k in range(cols)]
        for k in range(0, cols, 2):
            heads[k // 2, s] = last_in[k] + last_in[k + 1] * 65536
        return (o, *last_in)

    carry = (jnp.int32(-1),) + (jnp.int32(none),) * cols
    for g in range(chunks):
        if g == X_CHUNK:
            @pl.when(core == 0)
            def _():
                pl.semaphore_wait(barrier, 2 * (cols - 1) + 1)
                pl.semaphore_signal(x_ready, inc=1, device_id={"row": partner}, device_id_type=MESH)

            @pl.when(core == 1)
            def _():
                pl.semaphore_wait(x_ready, 1)

            first_copies = gather(0, 0, 0, sets)
        if g == Z_CHUNK:
            @pl.when(core == 1)
            def _():
                pl.semaphore_wait(barrier, 2 * (ring - 1) + 1)
                pl.semaphore_signal(z_ready, inc=1, device_id={"row": partner}, device_id_type=MESH)
        tile_copy(g).wait()
        if g + FLIGHT < chunks:
            tile_copy(g + FLIGHT).start()
        carry = lax.fori_loop(g * group, (g + 1) * group, add_tile, carry, unroll=4)

    used = count[0, 0]
    steps = [1 << b for b in reversed(range(slots.bit_length()))]

    def last_slots(o):
        end = jnp.int32(0)
        for step in steps:
            mid = end + step
            inside = mid <= used
            fits = outs[0, 0, jnp.minimum(mid, slots) - 1] <= o
            end = jnp.where(inside & fits, mid, end)
        at = jnp.maximum(end - 1, 0)
        hit = (end > 0) & (outs[0, 0, at] == o)
        found = []
        for k in range(0, cols, 2):
            pair = heads[k // 2, at]
            found.append(jnp.where(hit, pair % 65536, none))
            found.append(jnp.where(hit, pair // 65536, none))
        return found

    def target(n):
        return lax.rem(chip + order[n], ring)

    def build(n):
        for half in range(2):
            places = last_slots(target(n) * 2 + half)
            for k in range(cols):
                for q in range(PARTS):
                    value = sums[q][places[k]]
                    high = value.astype(jnp.bfloat16)
                    low = (value - high.astype(jnp.float32)).astype(jnp.bfloat16)
                    at = k * edge + q * part
                    w[n, at:at + part, half * edge:(half + 1) * edge] = high
                    w[n, depth + at:depth + at + part, half * edge:(half + 1) * edge] = low

    def multiply(x, n, step, half, at):
        both = jnp.dot(x, w[n], preferred_element_type=jnp.float32)
        left, right = both[:, :edge], both[:, edge:]
        rows_at = pl.ds(at, x.shape[0])
        psend[step, n, rows_at] = jnp.where(core == 0, right, left).astype(jnp.bfloat16)
        own[n, rows_at] = jnp.where(core == 0, left, right)
        if step == 0 and n + 1 < ring:
            build(n + 1)
        return send(
            psend.at[step, n, rows_at], precv.at[step, n, rows_at],
            ps_send.at[step, half, n], ps_recv.at[step, half, n], {"row": partner},
        )

    def add_partner(copy, n, step, at, length):
        copy.wait_recv()
        rows_at = pl.ds(at, length)
        total = own[n, rows_at] + precv[step, n, rows_at].astype(jnp.float32)
        if order[n] == 0:
            own[n, rows_at] = total
        else:
            zsend[step, n, rows_at] = total.astype(jnp.bfloat16)

    def send_chip(n, step, half):
        if order[n] == 0:
            return None
        rows_at = pl.ds(half * size, size)
        return send(
            zsend.at[step, n, rows_at], zrecv.at[step, n, rows_at],
            zs_send.at[step, half, n], zs_recv.at[step, half, n], {"row": target(n) * 2 + core},
        )

    def collect(copies, step, half):
        rows_at = pl.ds(half * size, size)
        total = own[ring - 1, rows_at]
        for n in reversed(range(ring - 1)):
            copies[n].wait_recv()
            total += zrecv[step, n, rows_at].astype(jnp.float32)
        return total

    def input_rows(step, at, length):
        parts = [xs[step, k, at:at + length] for k in range(cols)]
        return jnp.concatenate(parts + parts, axis=1)

    build(0)
    for copy in first_copies:
        copy.wait_recv()
    x = input_rows(0, 0, sets)
    pending = []
    chip_copies = [[None] * ring for _ in range(HALVES)]

    @pl.when(core == 0)
    def _():
        pl.semaphore_wait(z_ready, 1)

    def pass_on(step, halves, at, length):
        copy, n = pending.pop(0)
        add_partner(copy, n, step, at, length)
        chip_copies[halves][n] = send_chip(n, step, halves)

    for n in range(ring):
        pending.append((multiply(x, n, 0, 0, 0), n))
        if n >= LAG_FIRST:
            pass_on(0, 0, 0, sets)
    while pending:
        pass_on(0, 0, 0, sets)
    for half in range(1, HALVES):
        for n in range(ring):
            chip_copies[half][n] = send_chip(n, 0, half)

    local_ids = seeds[...].T - (row * cols + col) * edge
    places = lax.broadcasted_iota(jnp.int32, (sets, edge), 1)
    restart = jnp.zeros((sets, edge), jnp.float32)
    for j in range(local_ids.shape[1]):
        restart += (local_ids[:, j:j + 1] == places).astype(jnp.float32)
    prior[...] = (1.0 - damping) * restart

    col_copies = []
    for half in range(HALVES):
        rows_at = pl.ds(half * size, size)
        risk = prior[rows_at] + damping * collect(chip_copies[half], 0, half)
        xs[1, col, rows_at] = (risk / degrees).astype(jnp.bfloat16)
        col_copies.append(gather(1, half, half * size, size))

    chip_copies = [[None] * ring for _ in range(HALVES)]
    for half in range(HALVES):
        for copy in col_copies[half]:
            copy.wait_recv()
        x = input_rows(1, half * size, size)
        for n in range(ring):
            pending.append((multiply(x, n, 1, half, half * size), n))
            if n >= LAG_LAST:
                pass_on(1, half, half * size, size)
        while pending:
            pass_on(1, half, half * size, size)
    for half in range(HALVES):
        rows_at = pl.ds(half * size, size)
        risk_out[rows_at] = prior[rows_at] + damping * collect(chip_copies[half], 1, half)
    for copy in sent:
        copy.wait_send()


def local(tiles, tile_out, tile_in, tile_count, out_degree, seed_ids, prior):
    rows, cols = lax.axis_size("row"), lax.axis_size("col")
    slots, edge = tiles.shape[2], tiles.shape[4]
    sets = prior.shape[0]
    ring = rows // 2
    chunks = math.gcd(slots, CHUNKS)
    vmem = pl.BlockSpec(memory_space=pltpu.VMEM)
    hbm = pl.BlockSpec(memory_space=pltpu.HBM)
    block = (sets, edge)
    dma = pltpu.SemaphoreType.DMA
    return pl.pallas_call(
        functools.partial(kernel, rows, cols, chunks),
        out_shape=jax.ShapeDtypeStruct(block, jnp.float32),
        in_specs=[pl.BlockSpec(memory_space=pltpu.SMEM)] + [hbm] * 6,
        out_specs=vmem,
        scratch_shapes=[
            pltpu.SMEM(tile_out.shape, jnp.int32),
            pltpu.SMEM(tile_in.shape, jnp.int32),
            pltpu.VMEM((1, edge), jnp.int32),
            pltpu.VMEM(seed_ids.shape[::-1], jnp.int32),
            pltpu.VMEM(block, jnp.float32),
            pltpu.VMEM((slots, edge, edge), jnp.bfloat16),
            *[pltpu.VMEM((slots + 1, edge // PARTS, edge), jnp.float32) for _ in range(PARTS)],
            pltpu.SMEM((cols // 2, slots), jnp.int32),
            pltpu.VMEM((ring, 2 * cols * edge, 2 * edge), jnp.bfloat16),
            pltpu.VMEM((ITERATIONS, cols, *block), jnp.bfloat16),
            pltpu.VMEM((ring, *block), jnp.float32),
            pltpu.VMEM((ITERATIONS, ring, *block), jnp.bfloat16),
            pltpu.VMEM((ITERATIONS, ring, *block), jnp.bfloat16),
            pltpu.VMEM((ITERATIONS, ring, *block), jnp.bfloat16),
            pltpu.VMEM((ITERATIONS, ring, *block), jnp.bfloat16),
            dma((5,)),
            dma((chunks,)),
            dma((ITERATIONS, HALVES, cols)),
            dma((ITERATIONS, HALVES, cols)),
            dma((ITERATIONS, HALVES, ring)),
            dma((ITERATIONS, HALVES, ring)),
            dma((ITERATIONS, HALVES, ring)),
            dma((ITERATIONS, HALVES, ring)),
            pltpu.SemaphoreType.REGULAR,
            pltpu.SemaphoreType.REGULAR,
        ],
        compiler_params=pltpu.CompilerParams(
            collective_id=0, has_side_effects=True, vmem_limit_bytes=52 * 1024 * 1024
        ),
    )(
        tile_count,
        *[pltpu.with_memory_space_constraint(a, pltpu.HBM) for a in (
            tile_out,
            tile_in,
            tiles.reshape(slots, edge, edge),
            out_degree.reshape(1, edge),
            seed_ids.T,
            prior,
        )]
    )


def solution(mesh):
    placed = (
        P("row", "col", None, None, None),
        P("row", "col", None),
        P("row", "col", None),
        P("row", "col"),
        P(("row", "col")),
        P("seed", None),
        P("seed", ("row", "col")),
    )
    return jax.shard_map(
        local, mesh=mesh, in_specs=placed, out_specs=P("seed", ("row", "col")), check_vma=False
    )
```

time: 48.4 us -> 38.4 us (0.79)
  Pallas kernels: 42 us -> 37 us
  other arithmetic: 2.53 us -> 0 us
  local copies, waits for them, and re-layouts: 2.9 us -> 0.63 us
    pallas_call x1, Pallas kernels: 42 us -> 37 us  [local(): pl.pallas_call(functools.partial(kernel, rows, cols, chunks), out_shape=j...]
    unnamed x2 -> x0, other arithmetic: 2.53 us -> none
    unnamed x2 -> x1, local copies, waits for them, and re-layouts: 2.9 us -> 0.63 us
where the time goes in v2:
time: 38.4 us; the launch traced here: 38.3 us
  Pallas kernels  37 us (96%)
  between operations  0.66 us (2%)
  local copies, waits for them, and re-layouts  0.63 us (2%)
    pallas_call x1, Pallas kernels, local(): pl.pallas_call(functools.partial(kernel, rows, cols, chunks), out_shape=j...  37 us

profile of v2, /device:TPU:1, one launch (start us, length us, event | category | flops | bytes accessed | tf_op | source)
XLA Modules:
  0.0 38.3 jit_solution(16043297096488453208)
XLA Ops:
  0.7 37.0 %shard_map.73 = f32[128,128]{1,0:T(8,128)S(1)} custom-call(s32[1,1]{1,0:T(1,128)S(6)} %copy.9.count, s32[1,1,384]{2,1,0:T(1,128)} %outs_in.1, s32[1,1,384]{2,1,0:T(1,128)} %ins_in.1, bf16[384,128,128]{2,1,0:T(8,128)(2,1)} %bitcast.3, s32[1,128]{1,0:T(1,128)} %bitcast.5, s32[16,128]{1,0:T(8,128)} %bitcast.4, f32[128,128]{1,0:T(8,128)} %prior_in.1), custom_call_target="tpu_custom_call" | custom-call | tf_op jit(solution)/shard_map/pallas_call | solution.py:292
  37.7 0.6 %copy.10 = f32[128,128]{1,0:T(8,128)} copy(f32[128,128]{1,0:T(8,128)S(1)} %shard_map.73) | data formatting | bytes 131072

commit v3 on v2

--- a/solution.py
+++ b/solution.py
@@ -12,11 +12,10 @@
 PARTS = 4
 CHUNKS = 16
 FLIGHT = 4
-HALVES = 2
+PIECES = (8, 8)
 X_CHUNK = 2
 Z_CHUNK = 12
 LAG_FIRST = 3
-LAG_LAST = 5
 damping = 0.85
 MESH = pl.DeviceIdType.MESH
 
@@ -29,13 +28,17 @@
     rows, cols, chunks,
     count, outs_in, ins_in, tiles, degree_in, seeds_in, prior_in, risk_out,
     outs, ins, degree, seeds, prior, buf, sum0, sum1, sum2, sum3, heads,
-    w, xs, own, psend, precv, zsend, zrecv,
-    isem, tsem, xs_send, xs_recv, ps_send, ps_recv, zs_send, zs_recv, x_ready, z_ready,
+    w, w_other, xs, xs_last, own, psend, precv, zsend, zrecv,
+    isem, tsem, ws_send, ws_recv, xs_send, xs_recv, xl_send, xl_recv, ps_send, ps_recv, zs_send, zs_recv,
+    x_ready, z_ready,
 ):
     sums = (sum0, sum1, sum2, sum3)
     slots, edge, _ = buf.shape
     sets = prior.shape[0]
-    size = sets // HALVES
+    pieces = []
+    for share in PIECES:
+        size = sets * share // sum(PIECES)
+        pieces.append((pieces[-1][0] + pieces[-1][1] if pieces else 0, size))
     group = slots // chunks
     part = edge // PARTS
     ring = rows // 2
@@ -87,18 +90,27 @@
     small[1].wait()
     degrees = degree[...].astype(jnp.float32)
 
-    def gather(step, half, at, length):
-        rows_at = pl.ds(at, length)
+    def gather_first():
         return [
             send(
-                xs.at[step, col, rows_at], xs.at[step, col, rows_at],
-                xs_send.at[step, half, d - 1], xs_recv.at[step, half, d - 1],
+                xs.at[col], xs.at[col], xs_send.at[d - 1], xs_recv.at[d - 1],
                 {"col": lax.rem(col + d, cols)},
             )
             for d in range(1, cols)
         ]
 
-    xs[0, col] = (prior[...] / degrees).astype(jnp.bfloat16)
+    def gather_last(piece):
+        at, size = pieces[piece]
+        mine = xs_last.at[core, col, pl.ds(at, size)]
+        return [
+            send(
+                mine, mine, xl_send.at[piece, other, d], xl_recv.at[piece, other, d],
+                {"row": row if other == 0 else partner, "col": lax.rem(col + d, cols)},
+            )
+            for d in ring_order(cols) for other in range(2) if d + other > 0
+        ]
+
+    xs[col] = (prior[...] / degrees).astype(jnp.bfloat16)
     for copy in small[2:]:
         copy.wait()
     for q in range(PARTS):
@@ -133,7 +145,7 @@
             def _():
                 pl.semaphore_wait(x_ready, 1)
 
-            first_copies = gather(0, 0, 0, sets)
+            first_copies = gather_first()
         if g == Z_CHUNK:
             @pl.when(core == 1)
             def _():
@@ -175,77 +187,73 @@
                     high = value.astype(jnp.bfloat16)
                     low = (value - high.astype(jnp.float32)).astype(jnp.bfloat16)
                     at = k * edge + q * part
-                    w[n, at:at + part, half * edge:(half + 1) * edge] = high
-                    w[n, depth + at:depth + at + part, half * edge:(half + 1) * edge] = low
-
-    def multiply(x, n, step, half, at):
-        both = jnp.dot(x, w[n], preferred_element_type=jnp.float32)
-        left, right = both[:, :edge], both[:, edge:]
-        rows_at = pl.ds(at, x.shape[0])
-        psend[step, n, rows_at] = jnp.where(core == 0, right, left).astype(jnp.bfloat16)
-        own[n, rows_at] = jnp.where(core == 0, left, right)
-        if step == 0 and n + 1 < ring:
-            build(n + 1)
-        return send(
-            psend.at[step, n, rows_at], precv.at[step, n, rows_at],
-            ps_send.at[step, half, n], ps_recv.at[step, half, n], {"row": partner},
-        )
-
-    def add_partner(copy, n, step, at, length):
+                    w[n, half, at:at + part] = high
+                    w[n, half, depth + at:depth + at + part] = low
+
+    def add_partner(copy, n):
         copy.wait_recv()
-        rows_at = pl.ds(at, length)
-        total = own[n, rows_at] + precv[step, n, rows_at].astype(jnp.float32)
+        total = own[n] + precv[n].astype(jnp.float32)
         if order[n] == 0:
-            own[n, rows_at] = total
+            own[n] = total
         else:
-            zsend[step, n, rows_at] = total.astype(jnp.bfloat16)
-
-    def send_chip(n, step, half):
+            zsend[0, n] = total.astype(jnp.bfloat16)
+
+    def send_chip(n, step, piece):
         if order[n] == 0:
             return None
-        rows_at = pl.ds(half * size, size)
+        at, size = pieces[piece]
+        rows_at = pl.ds(at, size)
         return send(
             zsend.at[step, n, rows_at], zrecv.at[step, n, rows_at],
-            zs_send.at[step, half, n], zs_recv.at[step, half, n], {"row": target(n) * 2 + core},
+            zs_send.at[step, piece, n], zs_recv.at[step, piece, n], {"row": target(n) * 2 + core},
         )
 
-    def collect(copies, step, half):
-        rows_at = pl.ds(half * size, size)
+    def collect(copies, step, piece):
+        at, size = pieces[piece]
+        rows_at = pl.ds(at, size)
         total = own[ring - 1, rows_at]
         for n in reversed(range(ring - 1)):
             copies[n].wait_recv()
             total += zrecv[step, n, rows_at].astype(jnp.float32)
         return total
 
-    def input_rows(step, at, length):
-        parts = [xs[step, k, at:at + length] for k in range(cols)]
-        return jnp.concatenate(parts + parts, axis=1)
-
     build(0)
     for copy in first_copies:
         copy.wait_recv()
-    x = input_rows(0, 0, sets)
-    pending = []
-    chip_copies = [[None] * ring for _ in range(HALVES)]
+    parts = [xs[k] for k in range(cols)]
+    x = jnp.concatenate(parts + parts, axis=1)
+    chip_copies = [[None] * ring for _ in pieces]
 
     @pl.when(core == 0)
     def _():
         pl.semaphore_wait(z_ready, 1)
 
-    def pass_on(step, halves, at, length):
+    pending = []
+
+    def pass_on():
         copy, n = pending.pop(0)
-        add_partner(copy, n, step, at, length)
-        chip_copies[halves][n] = send_chip(n, step, halves)
+        add_partner(copy, n)
+        chip_copies[0][n] = send_chip(n, 0, 0)
 
     for n in range(ring):
-        pending.append((multiply(x, n, 0, 0, 0), n))
+        both = jnp.dot(x, jnp.concatenate([w[n, 0], w[n, 1]], axis=1), preferred_element_type=jnp.float32)
+        left, right = both[:, :edge], both[:, edge:]
+        psend[n] = jnp.where(core == 0, right, left).astype(jnp.bfloat16)
+        own[n] = jnp.where(core == 0, left, right)
+        if n + 1 < ring:
+            build(n + 1)
+        pending.append((send(psend.at[n], precv.at[n], ps_send.at[n], ps_recv.at[n], {"row": partner}), n))
         if n >= LAG_FIRST:
-            pass_on(0, 0, 0, sets)
+            pass_on()
     while pending:
-        pass_on(0, 0, 0, sets)
-    for half in range(1, HALVES):
+        pass_on()
+    for piece in range(1, len(pieces)):
         for n in range(ring):
-            chip_copies[half][n] = send_chip(n, 0, half)
+            chip_copies[piece][n] = send_chip(n, 0, piece)
+    w_copies = [
+        send(w.at[n, 1 - core], w_other.at[n], ws_send.at[n], ws_recv.at[n], {"row": partner})
+        for n in range(ring)
+    ]
 
     local_ids = seeds[...].T - (row * cols + col) * edge
     places = lax.broadcasted_iota(jnp.int32, (sets, edge), 1)
@@ -255,26 +263,44 @@
     prior[...] = (1.0 - damping) * restart
 
     col_copies = []
-    for half in range(HALVES):
-        rows_at = pl.ds(half * size, size)
-        risk = prior[rows_at] + damping * collect(chip_copies[half], 0, half)
-        xs[1, col, rows_at] = (risk / degrees).astype(jnp.bfloat16)
-        col_copies.append(gather(1, half, half * size, size))
-
-    chip_copies = [[None] * ring for _ in range(HALVES)]
-    for half in range(HALVES):
-        for copy in col_copies[half]:
+    for piece, (at, size) in enumerate(pieces):
+        rows_at = pl.ds(at, size)
+        risk = prior[rows_at] + damping * collect(chip_copies[piece], 0, piece)
+        xs_last[core, col, rows_at] = (risk / degrees).astype(jnp.bfloat16)
+        col_copies.append(gather_last(piece))
+
+    last_copies = [[None] * ring for _ in pieces]
+
+    def store(piece):
+        at, size = pieces[piece]
+        rows_at = pl.ds(at, size)
+        risk_out[rows_at] = prior[rows_at] + damping * collect(last_copies[piece], 1, piece)
+
+    for copy in w_copies:
+        copy.wait_recv()
+    for piece, (at, size) in enumerate(pieces):
+        rows_at = pl.ds(at, size)
+        for copy in col_copies[piece]:
             copy.wait_recv()
-        x = input_rows(1, half * size, size)
-        for n in range(ring):
-            pending.append((multiply(x, n, 1, half, half * size), n))
-            if n >= LAG_LAST:
-                pass_on(1, half, half * size, size)
-        while pending:
-            pass_on(1, half, half * size, size)
-    for half in range(HALVES):
-        rows_at = pl.ds(half * size, size)
-        risk_out[rows_at] = prior[rows_at] + damping * collect(chip_copies[half], 1, half)
+        near = [xs_last[core, k, rows_at] for k in range(cols)]
+        far = [xs_last[1 - core, k, rows_at] for k in range(cols)]
+        near = jnp.concatenate(near + near, axis=1)
+        far = jnp.concatenate(far + far, axis=1)
+        for n in range(0, ring, 2):
+            both = jnp.dot(
+                near, jnp.concatenate([w[n, core], w[n + 1, core]], axis=1), preferred_element_type=jnp.float32
+            ) + jnp.dot(
+                far, jnp.concatenate([w_other[n], w_other[n + 1]], axis=1), preferred_element_type=jnp.float32
+            )
+            for m, total in ((n, both[:, :edge]), (n + 1, both[:, edge:])):
+                if order[m] == 0:
+                    own[m, rows_at] = total
+                else:
+                    zsend[1, m, rows_at] = total.astype(jnp.bfloat16)
+            for m in (n, n + 1):
+                last_copies[piece][m] = send_chip(m, 1, piece)
+    for piece in range(len(pieces)):
+        store(piece)
     for copy in sent:
         copy.wait_send()
 
@@ -303,21 +329,27 @@
             pltpu.VMEM((slots, edge, edge), jnp.bfloat16),
             *[pltpu.VMEM((slots + 1, edge // PARTS, edge), jnp.float32) for _ in range(PARTS)],
             pltpu.SMEM((cols // 2, slots), jnp.int32),
-            pltpu.VMEM((ring, 2 * cols * edge, 2 * edge), jnp.bfloat16),
-            pltpu.VMEM((ITERATIONS, cols, *block), jnp.bfloat16),
+            pltpu.VMEM((ring, 2, 2 * cols * edge, edge), jnp.bfloat16),
+            pltpu.VMEM((ring, 2 * cols * edge, edge), jnp.bfloat16),
+            pltpu.VMEM((cols, *block), jnp.bfloat16),
+            pltpu.VMEM((2, cols, *block), jnp.bfloat16),
             pltpu.VMEM((ring, *block), jnp.float32),
-            pltpu.VMEM((ITERATIONS, ring, *block), jnp.bfloat16),
-            pltpu.VMEM((ITERATIONS, ring, *block), jnp.bfloat16),
+            pltpu.VMEM((ring, *block), jnp.bfloat16),
+            pltpu.VMEM((ring, *block), jnp.bfloat16),
             pltpu.VMEM((ITERATIONS, ring, *block), jnp.bfloat16),
             pltpu.VMEM((ITERATIONS, ring, *block), jnp.bfloat16),
             dma((5,)),
             dma((chunks,)),
-            dma((ITERATIONS, HALVES, cols)),
-            dma((ITERATIONS, HALVES, cols)),
-            dma((ITERATIONS, HALVES, ring)),
-            dma((ITERATIONS, HALVES, ring)),
-            dma((ITERATIONS, HALVES, ring)),
-            dma((ITERATIONS, HALVES, ring)),
+            dma((ring,)),
+            dma((ring,)),
+            dma((cols,)),
+            dma((cols,)),
+            dma((len(PIECES), 2, cols)),
+            dma((len(PIECES), 2, cols)),
+            dma((ring,)),
+            dma((ring,)),
+            dma((ITERATIONS, len(PIECES), ring)),
+            dma((ITERATIONS, len(PIECES), ring)),
             pltpu.SemaphoreType.REGULAR,
             pltpu.SemaphoreType.REGULAR,
         ],

time: 38.4 us -> 36.1 us (0.940)
  Pallas kernels: 37 us -> 34.7 us
    pallas_call x1, Pallas kernels: 37 us -> 34.7 us  [local(): pl.pallas_call(functools.partial(kernel, rows, cols, chunks), out_shape=j...]
where the time goes in v3:
time: 36.1 us; the launch traced here: 36 us
  Pallas kernels  34.7 us (96%)
  between operations  0.66 us (2%)
  local copies, waits for them, and re-layouts  0.63 us (2%)
    pallas_call x1, Pallas kernels, local(): pl.pallas_call(functools.partial(kernel, rows, cols, chunks), out_shape=j...  34.7 us

profile of v3, /device:TPU:1, one launch (start us, length us, event | category | flops | bytes accessed | tf_op | source)
XLA Modules:
  0.0 36.0 jit_solution(16690921240213407080)
XLA Ops:
  0.7 34.7 %shard_map.73 = f32[128,128]{1,0:T(8,128)S(1)} custom-call(s32[1,1]{1,0:T(1,128)S(6)} %copy.9.count, s32[1,1,384]{2,1,0:T(1,128)} %outs_in.1, s32[1,1,384]{2,1,0:T(1,128)} %ins_in.1, bf16[384,128,128]{2,1,0:T(8,128)(2,1)} %bitcast.3, s32[1,128]{1,0:T(1,128)} %bitcast.5, s32[16,128]{1,0:T(8,128)} %bitcast.4, f32[128,128]{1,0:T(8,128)} %prior_in.1), custom_call_target="tpu_custom_call" | custom-call | tf_op jit(solution)/shard_map/pallas_call | solution.py:318
  35.4 0.6 %copy.10 = f32[128,128]{1,0:T(8,128)} copy(f32[128,128]{1,0:T(8,128)S(1)} %shard_map.73) | data formatting | bytes 131072

commit v4 on v3

--- a/solution.py
+++ b/solution.py
@@ -15,7 +15,7 @@
 PIECES = (8, 8)
 X_CHUNK = 2
 Z_CHUNK = 12
-LAG_FIRST = 3
+LAG_FIRST = 2
 damping = 0.85
 MESH = pl.DeviceIdType.MESH
 
@@ -251,7 +251,7 @@
         for n in range(ring):
             chip_copies[piece][n] = send_chip(n, 0, piece)
     w_copies = [
-        send(w.at[n, 1 - core], w_other.at[n], ws_send.at[n], ws_recv.at[n], {"row": partner})
+        send(w.at[n, 1 - core, pl.ds(0, depth)], w_other.at[n], ws_send.at[n], ws_recv.at[n], {"row": partner})
         for n in range(ring)
     ]
 
@@ -284,14 +284,11 @@
             copy.wait_recv()
         near = [xs_last[core, k, rows_at] for k in range(cols)]
         far = [xs_last[1 - core, k, rows_at] for k in range(cols)]
-        near = jnp.concatenate(near + near, axis=1)
-        far = jnp.concatenate(far + far, axis=1)
+        x = jnp.concatenate(near + far, axis=1)
         for n in range(0, ring, 2):
-            both = jnp.dot(
-                near, jnp.concatenate([w[n, core], w[n + 1, core]], axis=1), preferred_element_type=jnp.float32
-            ) + jnp.dot(
-                far, jnp.concatenate([w_other[n], w_other[n + 1]], axis=1), preferred_element_type=jnp.float32
-            )
+            mine = jnp.concatenate([w[n, core, :depth], w[n + 1, core, :depth]], axis=1)
+            other = jnp.concatenate([w_other[n], w_other[n + 1]], axis=1)
+            both = jnp.dot(x, jnp.concatenate([mine, other], axis=0), preferred_element_type=jnp.float32)
             for m, total in ((n, both[:, :edge]), (n + 1, both[:, edge:])):
                 if order[m] == 0:
                     own[m, rows_at] = total
@@ -330,7 +327,7 @@
             *[pltpu.VMEM((slots + 1, edge // PARTS, edge), jnp.float32) for _ in range(PARTS)],
             pltpu.SMEM((cols // 2, slots), jnp.int32),
             pltpu.VMEM((ring, 2, 2 * cols * edge, edge), jnp.bfloat16),
-            pltpu.VMEM((ring, 2 * cols * edge, edge), jnp.bfloat16),
+            pltpu.VMEM((ring, cols * edge, edge), jnp.bfloat16),
             pltpu.VMEM((cols, *block), jnp.bfloat16),
             pltpu.VMEM((2, cols, *block), jnp.bfloat16),
             pltpu.VMEM((ring, *block), jnp.float32),

time: 36.1 us -> 35.5 us (0.983)
  Pallas kernels: 34.7 us -> 34.1 us
    pallas_call x1, Pallas kernels: 34.7 us -> 34.1 us  [local(): pl.pallas_call(functools.partial(kernel, rows, cols, chunks), out_shape=j...]
where the time goes in v4:
time: 35.5 us; the launch traced here: 35.4 us
  Pallas kernels  34.1 us (96%)
  between operations  0.66 us (2%)
  local copies, waits for them, and re-layouts  0.63 us (2%)
    pallas_call x1, Pallas kernels, local(): pl.pallas_call(functools.partial(kernel, rows, cols, chunks), out_shape=j...  34.1 us

profile of v4, /device:TPU:1, one launch (start us, length us, event | category | flops | bytes accessed | tf_op | source)
XLA Modules:
  0.0 35.4 jit_solution(14427356436827534223)
XLA Ops:
  0.7 34.1 %shard_map.73 = f32[128,128]{1,0:T(8,128)S(1)} custom-call(s32[1,1]{1,0:T(1,128)S(6)} %copy.9.count, s32[1,1,384]{2,1,0:T(1,128)} %outs_in.1, s32[1,1,384]{2,1,0:T(1,128)} %ins_in.1, bf16[384,128,128]{2,1,0:T(8,128)(2,1)} %bitcast.3, s32[1,128]{1,0:T(1,128)} %bitcast.5, s32[16,128]{1,0:T(8,128)} %bitcast.4, f32[128,128]{1,0:T(8,128)} %prior_in.1), custom_call_target="tpu_custom_call" | custom-call | tf_op jit(solution)/shard_map/pallas_call | solution.py:315
  34.7 0.6 %copy.10 = f32[128,128]{1,0:T(8,128)} copy(f32[128,128]{1,0:T(8,128)S(1)} %shard_map.73) | data formatting | bytes 131072

commit v5 on v4

--- a/solution.py
+++ b/solution.py
@@ -250,11 +250,6 @@
     for piece in range(1, len(pieces)):
         for n in range(ring):
             chip_copies[piece][n] = send_chip(n, 0, piece)
-    w_copies = [
-        send(w.at[n, 1 - core, pl.ds(0, depth)], w_other.at[n], ws_send.at[n], ws_recv.at[n], {"row": partner})
-        for n in range(ring)
-    ]
-
     local_ids = seeds[...].T - (row * cols + col) * edge
     places = lax.broadcasted_iota(jnp.int32, (sets, edge), 1)
     restart = jnp.zeros((sets, edge), jnp.float32)
@@ -268,6 +263,11 @@
         risk = prior[rows_at] + damping * collect(chip_copies[piece], 0, piece)
         xs_last[core, col, rows_at] = (risk / degrees).astype(jnp.bfloat16)
         col_copies.append(gather_last(piece))
+        if piece == 0:
+            w_copies = [
+                send(w.at[n, 1 - core, pl.ds(0, depth)], w_other.at[n], ws_send.at[n], ws_recv.at[n], {"row": partner})
+                for n in range(ring)
+            ]
 
     last_copies = [[None] * ring for _ in pieces]
 

time: 35.5 us -> 35.6 us (level)
  no operation moved by 1% of the time
where the time goes in v5:
time: 35.6 us; the launch traced here: 35.5 us
  Pallas kernels  34.2 us (96%)
  between operations  0.66 us (2%)
  local copies, waits for them, and re-layouts  0.63 us (2%)
    pallas_call x1, Pallas kernels, local(): pl.pallas_call(functools.partial(kernel, rows, cols, chunks), out_shape=j...  34.2 us

profile of v5, /device:TPU:1, one launch (start us, length us, event | category | flops | bytes accessed | tf_op | source)
XLA Modules:
  0.0 35.5 jit_solution(16782474144668713386)
XLA Ops:
  0.7 34.2 %shard_map.73 = f32[128,128]{1,0:T(8,128)S(1)} custom-call(s32[1,1]{1,0:T(1,128)S(6)} %copy.9.count, s32[1,1,384]{2,1,0:T(1,128)} %outs_in.1, s32[1,1,384]{2,1,0:T(1,128)} %ins_in.1, bf16[384,128,128]{2,1,0:T(8,128)(2,1)} %bitcast.3, s32[1,128]{1,0:T(1,128)} %bitcast.5, s32[16,128]{1,0:T(8,128)} %bitcast.4, f32[128,128]{1,0:T(8,128)} %prior_in.1), custom_call_target="tpu_custom_call" | custom-call | tf_op jit(solution)/shard_map/pallas_call | solution.py:315
  34.9 0.6 %copy.10 = f32[128,128]{1,0:T(8,128)} copy(f32[128,128]{1,0:T(8,128)S(1)} %shard_map.73) | data formatting | bytes 131072
